TPU v7x, 256 devices: a whole 4x4x8 slice. The times are simulated.
256 devices in a mesh: group: 4 (over x), dev: 64 (over y, z, core).
Axes of the slice: x: 4, y: 4, z: 8, core: 2. Of those that a mesh axis runs over, the one named last changes fastest.
Arguments:
- species: float32 [6, 512, 32768], P(None, ('group', 'dev')), may hold values from 0.5 to 2
- potential: float32 [512, 32768], P(('group', 'dev')), may hold values from -4 to 4
- pore: int32 [512, 32768], P(('group', 'dev')), may hold values 0 or 1
- openness: float32 [512, 32768], P(('group', 'dev')), may hold values from 0.3 to 1
- neighbours: int32 [512, 6], P(('group', 'dev')), may hold values from 0 to 1
- diffusivity: float32 [6], replicated, may hold values from 0.02 to 0.12
- rate_const: float32 [512], P(('group', 'dev')), may hold values from 0.1 to 1
- opened: int32 [512], P(('group', 'dev')), may hold values 0 or 1
- partner: int32 [256], P(('group', 'dev')), may hold values from 0 to 255, as said below
- give_slot: int32 [256], P(('group', 'dev')), may hold values from 0 to 1
Outputs:
- new_species: float32 [6, 512, 32768], P(None, ('group', 'dev'))
- new_potential: float32 [512, 32768], P(('group', 'dev'))
Inputs may be any that keep to these rules, and one draw needn't show every extreme that they name: partner[partner[q]] = q for every device q; a partner other than q differs from q in exactly one bit of the device index; over all devices at most two distinct bits occur, at most one of them below 64.
All inputs are finite; a program needn't handle non-finite values. No bound on the sum of `pore` or of `opened` on one device may be relied on, other than what follows from the above.
Results may differ from a plain program's by a relative error of at most 0.00002.
Values sent between devices are 32-bit elements; how exact they have to be, the bound alone decides.
A program may use at most 128 MiB of HBM per device.

v0:
```python
from functools import partial

import jax
import jax.numpy as jnp
from jax import lax
from jax.sharding import PartitionSpec as P

SIDE = 32
SWEEPS = 8


charge_scale = 0.5
screening = 0.5
solubility = 2.0
valences = (2.0, -1.0, 1.0, -1.0, 1.0, 2.0)
reaction_signs = (1.0, 1.0, -1.0, 0.0, 0.0, 0.0)


def passed_along(block, axis, distance):
    devices = range(lax.axis_size(axis))
    route = [((i - distance) % len(devices), i) for i in devices]
    return lax.ppermute(block, axis, route)


def partner_2(value, axis, apart):
    mask = 2**apart
    pairs = [(source, source ^ mask) for source in range(lax.axis_size(axis))]
    return lax.ppermute(value, axis, pairs)


def face_list(field):
    brick_side = field.shape[-2]
    cube_view = field.reshape(field.shape[:-1] + (brick_side, brick_side))
    flat_shape = field.shape[:-2] + (brick_side * brick_side,)
    return (
        field[..., 0, :],
        field[..., brick_side - 1, :],
        cube_view[..., :, 0, :].reshape(flat_shape),
        cube_view[..., :, brick_side - 1, :].reshape(flat_shape),
        cube_view[..., 0].reshape(flat_shape),
        cube_view[..., brick_side - 1].reshape(flat_shape),
    )


def beside_values(field, halo_list):
    brick_side = field.shape[-2]
    plane_shape = field.shape[:-2] + (brick_side, brick_side)
    cube_shape = field.shape[:-2] + (brick_side, brick_side, brick_side)
    east_side = jnp.concatenate([field[..., 1:, :], halo_list[0][..., None, :]], axis=-2)
    west_side = jnp.concatenate([halo_list[1][..., None, :], field[..., :-1, :]], axis=-2)
    north_side = jnp.concatenate(
        [field[..., brick_side:], halo_list[2].reshape(plane_shape)], axis=-1
    )
    south_side = jnp.concatenate(
        [halo_list[3].reshape(plane_shape), field[..., :-brick_side]], axis=-1
    )
    depth_index = jnp.arange(brick_side * brick_side, dtype=jnp.int32) % brick_side
    upper_rim = jnp.broadcast_to(halo_list[4].reshape(plane_shape)[..., None], cube_shape).reshape(
        field.shape
    )
    lower_rim = jnp.broadcast_to(halo_list[5].reshape(plane_shape)[..., None], cube_shape).reshape(
        field.shape
    )
    upper_side = jnp.where(
        depth_index == brick_side - 1,
        upper_rim,
        jnp.concatenate([field[..., 1:], field[..., :1]], axis=-1),
    )
    lower_side = jnp.where(
        depth_index == 0, lower_rim, jnp.concatenate([field[..., -1:], field[..., :-1]], axis=-1)
    )
    return (east_side, west_side, north_side, south_side, upper_side, lower_side)


def relax(nearby, density):
    total = nearby[0] + nearby[1] + nearby[2] + nearby[3] + nearby[4] + nearby[5] + density
    return total / (6.0 + screening)


def local_update(
    species,
    swept,
    wetted,
    pore_float,
    halo_species,
    halo_swept,
    halo_wetted,
    diffusivity,
    reactivity,
):
    near_swept = beside_values(swept, halo_swept)
    near_wetted = beside_values(wetted, halo_wetted)
    conductances = tuple((wetted * near_wetted[direction] for direction in range(6)))
    differences = tuple((swept - near_swept[direction] for direction in range(6)))
    reaction = (
        reactivity[:, None, None] * pore_float * (species[2] - species[0] * species[1] / solubility)
    )
    half_charge = 0.5 * jnp.asarray(valences, jnp.float32)
    signs = jnp.asarray(reaction_signs, jnp.float32)
    stacked_halos = jnp.stack(halo_species, axis=1)

    def ion_update(packed):
        conc, halos, half, rate, sign = packed
        near = beside_values(conc, tuple((halos[direction] for direction in range(6))))
        outflow = jnp.zeros_like(conc)
        for direction in range(6):
            outflow = outflow + conductances[direction] * (
                conc - near[direction] + half * (conc + near[direction]) * differences[direction]
            )
        return conc - rate * outflow + sign * reaction

    return lax.map(ion_update, (species, stacked_halos, half_charge, diffusivity, signs))


def sweep_along_dev(payload, offset):
    return passed_along(payload, "dev", offset)


def sweep_along_group(payload, offset):
    return passed_along(payload, "group", offset)


def carry_along_dev(payload, offset):
    return passed_along(payload, "dev", offset)


def carry_along_group(payload, offset):
    return passed_along(payload, "group", offset)


def collect_halos(face_sets, neighbours, along_dev, along_group, stride):
    moves = (
        (along_dev, -1),
        (along_dev, 1),
        (along_dev, -stride),
        (along_dev, stride),
        (along_group, -1),
        (along_group, 1),
    )
    collected = []
    for direction in range(6):
        mover, offset = moves[direction]
        arrived = mover(face_sets[direction], offset)
        chosen = neighbours[:, direction]
        collected.append(jax.tree.map(lambda payload: jnp.take(payload, chosen, axis=-2), arrived))
    return collected


def swap_pair(payload, bit_number):
    return partner_2(payload, ("group", "dev"), bit_number)


def keep_pair(payload):
    return payload


def local(
    species,
    potential,
    pore,
    openness,
    neighbours,
    diffusivity,
    rate_const,
    opened,
    partner,
    give_slot,
):
    brick_count = species.shape[1]
    ion_count = species.shape[0]
    cell_shape = (brick_count, SIDE, SIDE * SIDE)
    dev_count = lax.axis_size("dev")
    stride = dev_count // 4
    species_cube = species.reshape((ion_count,) + cell_shape)
    pore_float = pore.astype(jnp.float32).reshape(cell_shape)
    wetted = pore_float * openness.reshape(cell_shape)
    charges = jnp.asarray(valences, jnp.float32)[:, None, None, None]
    density = charge_scale * wetted * jnp.sum(charges * species_cube, axis=0)
    swept = potential.reshape(cell_shape)
    for sweep_index in range(SWEEPS):
        halo_list = collect_halos(
            face_list(swept), neighbours, sweep_along_dev, sweep_along_group, stride
        )
        swept = relax(beside_values(swept, tuple(halo_list)), density)
    face_sets = tuple(zip(face_list(species_cube), face_list(swept), face_list(wetted)))
    collected = collect_halos(face_sets, neighbours, carry_along_dev, carry_along_group, stride)
    reactivity = rate_const * opened.astype(jnp.float32)
    updated = local_update(
        species_cube,
        swept,
        wetted,
        pore_float,
        tuple((entry[0] for entry in collected)),
        tuple((entry[1] for entry in collected)),
        tuple((entry[2] for entry in collected)),
        diffusivity,
        reactivity,
    )
    own_index = lax.axis_index("group") * dev_count + lax.axis_index("dev")
    partner_index = partner[0]
    given_slot = give_slot[0]
    outgoing = (
        lax.dynamic_index_in_dim(updated, given_slot, 1, False),
        lax.dynamic_index_in_dim(swept, given_slot, 0, False),
    )
    received = outgoing
    bit_total = (lax.axis_size("group") * dev_count).bit_length() - 1
    powers = jnp.left_shift(jnp.int32(1), jnp.arange(bit_total, dtype=jnp.int32))
    flags = (jnp.bitwise_xor(partner_index, own_index) == powers).astype(jnp.int32)
    used = lax.pmax(flags, ("group", "dev"))
    for bit_number in range(bit_total):
        arrived = lax.cond(
            used[bit_number] > 0, partial(swap_pair, bit_number=bit_number), keep_pair, outgoing
        )
        incoming = partner_index == jnp.bitwise_xor(own_index, 1 << bit_number)
        received = (
            jnp.where(incoming, arrived[0], received[0]),
            jnp.where(incoming, arrived[1], received[1]),
        )
    new_species = lax.dynamic_update_index_in_dim(updated, received[0], given_slot, 1)
    new_potential = lax.dynamic_update_index_in_dim(swept, received[1], given_slot, 0)
    return (
        new_species.reshape(ion_count, brick_count, SIDE * SIDE * SIDE),
        new_potential.reshape(brick_count, SIDE * SIDE * SIDE),
    )


def solution(mesh):
    in_specs = (
        P(None, ("group", "dev"), None),
        P(("group", "dev"), None),
        P(("group", "dev"), None),
        P(("group", "dev"), None),
        P(("group", "dev"), None),
        P(),
        P(("group", "dev")),
        P(("group", "dev")),
        P(("group", "dev")),
        P(("group", "dev")),
    )
    out_specs = (P(None, ("group", "dev"), None), P(("group", "dev"), None))
    return jax.shard_map(local, mesh=mesh, in_specs=in_specs, out_specs=out_specs, check_vma=False)
```

profile of v0, /device:TPU:2, one launch (start us, length us, event | category | flops | bytes accessed | tf_op | source)
XLA Modules:
  0.0 721.6 jit_solution(9647291506013529839)
XLA Ops:
  1.9 7.7 %collective-permute-start.23 = (f32[2,1024]{1,0:T(2,128)}, f32[2,1024]{1,0:T(2,128)S(1)}, u32[]{:S(2)}, u32[]{:S(2)}) collective-permute-start(f32[2,1024]{1,0:T(2,128)} %get-tuple-element.927), channel_id=1, source_target_pairs={{1,0},{2,1},{3,2},{4,3},{5,4},{6,5},{7,6},{8,7},{9,8},{10,9},{11,1... | collective-permute-start | bytes 24584 | tf_op jit(solution)/shard_map/ppermute | solution.py:22
  26.9 4.9 reshape_reshape.6
  34.8 10.3 %slice_reduce_fusion = (f32[6,2,32,32]{3,2,1,0:T(8,128)}, f32[6,2,32,32]{3,2,1,0:T(8,128)}) fusion(f32[6,2,32,32,32]{4,3,2,1,0:T(8,128)} %reshape_reshape.6), kind=kLoop, calls=%fused_computation.123 | loop fusion | bytes 196608 | tf_op jit(solution)/shard_map/slice | solution.py:41
  53.4 78.6 %pmax.7 = s32[8]{0:T(128)S(1)} all-reduce(s32[8]{0:T(128)S(1)} %compare_convert_fusion), channel_id=1, replica_groups=mesh['group'=4,'dev'=64] {'group','dev'}, use_global_device_ids=true, to_apply=%region_3.6 | all-reduce | flops 8 | bytes 64 | tf_op jit(solution)/shard_map/pmax | solution.py:210
  186.7 3.6 fusion.30
  207.1 5.0 collective-permute-done.30
  217.7 5.1 collective-permute-start.16
  259.3 5.0 collective-permute-done.36
  332.8 3.6 fusion.121
  362.1 5.0 collective-permute-done.48
  425.1 4.1 collective-permute-done.56
  480.3 4.6 collective-permute-done.60
  493.4 3.7 fusion.118
  523.2 5.4 collective-permute-start.65
  556.4 5.4 collective-permute-start.71
  593.9 87.3 %while.13 = (s32[]{:T(128)}, f32[6,2,32,1024]{3,2,1,0:T(8,128)}, f32[6,2,32,1024]{3,2,1,0:T(8,128)}, f32[6]{0:T(128)}, f32[2,32,1024]{2,1,0:T(8,128)}, /*index=5...) while((s32[]{:T(128)}, f32[6,2,32,1024]{3,2,1,0:T(8,128)}, ...), condition=%wide.region_2.5_spmd.clone, body=%wide.region_1.4_spmd.sunk.clone.sunk | while | flops 3481607 | bytes 11524457 | solution.py:112
  603.6 4.9 fusion.214
  618.1 4.9 fusion.214
  632.7 4.9 fusion.214
  647.2 4.9 fusion.214
  661.8 4.9 fusion.214
  676.3 4.9 fusion.214
  682.4 18.3 %conditional.9 = (f32[6,32,1024]{2,1,0:T(8,128)}, f32[32,1024]{1,0:T(8,128)}) conditional(s32[]{:T(128)} %bitcast.79, (f32[6,32,1024]{2,1,0:T(8,128)S(1)}, f32[32,1024]{1,0:T(8,128)S(1)}) %tuple.345, (f32[6,32,1024]{2,1,0:T(8,128)S(1)}, f32[32,1024]{1,0:T(8,128)S(1)}) %tuple.346), branch_computations={%region_6.9_spmd, %region_7.10_spmd} | conditional | bytes 3670112 | solution.py:212
  685.6 15.1 %collective-permute-done.3 = f32[32,1024]{1,0:T(8,128)} collective-permute-done((f32[32,1024]{1,0:T(8,128)S(1)}, f32[32,1024]{1,0:T(8,128)}, u32[]{:S(2)}, u32[]{:S(2)}) %collective-permute-start.3) | collective-permute-done | bytes 131104 | tf_op jit(solution)/shard_map/cond/branch_1_fun/ppermute | solution.py:28
  (929 shorter events, 527.5 us)
Async XLA Ops:
  1.9 149.6 %collective-permute-start.23 = (f32[2,1024]{1,0:T(2,128)}, f32[2,1024]{1,0:T(2,128)S(1)}, u32[]{:S(2)}, u32[]{:S(2)}) collective-permute-start(f32[2,1024]{1,0:T(2,128)} %get-tuple-element.927), channel_id=1, source_target_pairs={{1,0},{2,1},{3,2},{4,3},{5,4},{6,5},{7,6},{8,7},{9,8},{10,9},{11,1... | collective-permute-start | bytes 24584 | tf_op jit(solution)/shard_map/ppermute | solution.py:22
  9.7 143.9 %collective-permute-start.24 = (f32[2,1024]{1,0:T(2,128)}, f32[2,1024]{1,0:T(2,128)S(1)}, u32[]{:S(2)}, u32[]{:S(2)}) collective-permute-start(f32[2,1024]{1,0:T(2,128)} %get-tuple-element.928), channel_id=1, source_target_pairs={{63,0},{0,1},{1,2},{2,3},{3,4},{4,5},{5,6},{6,7},{7,8},{8,9},{9,10... | collective-permute-start | bytes 24584 | tf_op jit(solution)/shard_map/ppermute | solution.py:22
  12.8 144.8 %collective-permute-start.27 = (f32[2,1024]{1,0:T(2,128)}, f32[2,1024]{1,0:T(2,128)S(1)}, u32[]{:S(2)}, u32[]{:S(2)}) collective-permute-start(f32[2,1024]{1,0:T(2,128)} %reshape_squeeze.138), channel_id=1, source_target_pairs={{64,0},{128,64},{192,128},{0,192},{65,1},{129,65},{193,129},{1,193... | collective-permute-start | bytes 24584 | tf_op jit(solution)/shard_map/ppermute | solution.py:22
  14.0 146.1 %collective-permute-start.28 = (f32[2,1024]{1,0:T(2,128)}, f32[2,1024]{1,0:T(2,128)S(1)}, u32[]{:S(2)}, u32[]{:S(2)}) collective-permute-start(f32[2,1024]{1,0:T(2,128)} %reshape_squeeze.139), channel_id=1, source_target_pairs={{192,0},{0,64},{64,128},{128,192},{193,1},{1,65},{65,129},{129,193... | collective-permute-start | bytes 24584 | tf_op jit(solution)/shard_map/ppermute | solution.py:22
  16.8 144.4 %collective-permute-start.25 = (f32[2,1024]{1,0:T(2,128)}, f32[2,1024]{1,0:T(2,128)S(1)}, u32[]{:S(2)}, u32[]{:S(2)}) collective-permute-start(f32[2,1024]{1,0:T(2,128)} %reshape_squeeze.136), channel_id=1, source_target_pairs={{16,0},{17,1},{18,2},{19,3},{20,4},{21,5},{22,6},{23,7},{24,8},{25... | collective-permute-start | bytes 24584 | tf_op jit(solution)/shard_map/ppermute | solution.py:22
  153.6 42.4 %collective-permute-start.78 = (f32[2,1024]{1,0:T(2,128)}, f32[2,1024]{1,0:T(2,128)S(1)}, u32[]{:S(2)}, u32[]{:S(2)}) collective-permute-start(f32[2,1024]{1,0:T(2,128)} %reshape_squeeze.172), channel_id=1, source_target_pairs={{64,0},{128,64},{192,128},{0,192},{65,1},{129,65},{193,129},{1,193... | collective-permute-start | bytes 24584 | tf_op jit(solution)/shard_map/ppermute | solution.py:22
  157.6 41.8 %collective-permute-start.74 = (f32[2,1024]{1,0:T(2,128)}, f32[2,1024]{1,0:T(2,128)S(1)}, u32[]{:S(2)}, u32[]{:S(2)}) collective-permute-start(f32[2,1024]{1,0:T(2,128)} %reshape_squeeze.168), channel_id=1, source_target_pairs={{16,0},{17,1},{18,2},{19,3},{20,4},{21,5},{22,6},{23,7},{24,8},{25... | collective-permute-start | bytes 24584 | tf_op jit(solution)/shard_map/ppermute | solution.py:22
  160.1 40.6 %collective-permute-start.76 = (f32[2,1024]{1,0:T(2,128)}, f32[2,1024]{1,0:T(2,128)S(1)}, u32[]{:S(2)}, u32[]{:S(2)}) collective-permute-start(f32[2,1024]{1,0:T(2,128)} %reshape_squeeze.170), channel_id=1, source_target_pairs={{48,0},{49,1},{50,2},{51,3},{52,4},{53,5},{54,6},{55,7},{56,8},{57... | collective-permute-start | bytes 24584 | tf_op jit(solution)/shard_map/ppermute | solution.py:22
  161.2 42.4 %collective-permute-start.80 = (f32[2,1024]{1,0:T(2,128)}, f32[2,1024]{1,0:T(2,128)S(1)}, u32[]{:S(2)}, u32[]{:S(2)}) collective-permute-start(f32[2,1024]{1,0:T(2,128)} %reshape_squeeze.174), channel_id=1, source_target_pairs={{192,0},{0,64},{64,128},{128,192},{193,1},{1,65},{65,129},{129,193... | collective-permute-start | bytes 24584 | tf_op jit(solution)/shard_map/ppermute | solution.py:22
  196.0 255.6 %collective-permute-start.17 = (f32[6,2,1024]{2,0,1:T(8,128)}, f32[6,2,1024]{2,0,1:T(8,128)}, u32[]{:S(2)}, u32[]{:S(2)}) collective-permute-start(f32[6,2,1024]{2,0,1:T(8,128)} %bitcast.427), channel_id=1, source_target_pairs={{1,0},{2,1},{3,2},{4,3},{5,4},{6,5},{7,6},{8,7},{9,8},{10,9},{11,1... | collective-permute-start | bytes 147464 | tf_op jit(solution)/shard_map/ppermute | solution.py:22
  199.4 258.7 %collective-permute-start.18 = (f32[6,2,1024]{2,0,1:T(8,128)}, f32[6,2,1024]{2,0,1:T(8,128)}, u32[]{:S(2)}, u32[]{:S(2)}) collective-permute-start(f32[6,2,1024]{2,0,1:T(8,128)} %bitcast.426), channel_id=1, source_target_pairs={{63,0},{0,1},{1,2},{2,3},{3,4},{4,5},{5,6},{6,7},{7,8},{8,9},{9,10... | collective-permute-start | bytes 147464 | tf_op jit(solution)/shard_map/ppermute | solution.py:22
  216.9 36.4 %collective-permute-start.72 = (f32[2,1024]{1,0:T(2,128)}, f32[2,1024]{1,0:T(2,128)S(1)}, u32[]{:S(2)}, u32[]{:S(2)}) collective-permute-start(f32[2,1024]{1,0:T(2,128)} %get-tuple-element.845), channel_id=1, source_target_pairs={{63,0},{0,1},{1,2},{2,3},{3,4},{4,5},{5,6},{6,7},{7,8},{8,9},{9,10... | collective-permute-start | bytes 24584 | tf_op jit(solution)/shard_map/ppermute | solution.py:22
  217.7 36.9 %collective-permute-start.16 = (f32[2,1024]{1,0:T(2,128)}, f32[2,1024]{1,0:T(2,128)S(1)}, u32[]{:S(2)}, u32[]{:S(2)}) collective-permute-start(f32[2,1024]{1,0:T(2,128)} %get-tuple-element.846), channel_id=1, source_target_pairs={{1,0},{2,1},{3,2},{4,3},{5,4},{6,5},{7,6},{8,7},{9,8},{10,9},{11,1... | collective-permute-start | bytes 24584 | tf_op jit(solution)/shard_map/ppermute | solution.py:22
  253.3 209.1 %collective-permute-start.19 = (f32[6,2,1024]{2,0,1:T(8,128)}, f32[6,2,1024]{2,0,1:T(8,128)}, u32[]{:S(2)}, u32[]{:S(2)}) collective-permute-start(f32[6,2,1024]{2,0,1:T(8,128)} %copy.750), channel_id=1, source_target_pairs={{16,0},{17,1},{18,2},{19,3},{20,4},{21,5},{22,6},{23,7},{24,8},{25... | collective-permute-start | bytes 147464 | tf_op jit(solution)/shard_map/ppermute | solution.py:22
  254.6 210.4 %collective-permute-start.20 = (f32[6,2,1024]{2,0,1:T(8,128)}, f32[6,2,1024]{2,0,1:T(8,128)}, u32[]{:S(2)}, u32[]{:S(2)}) collective-permute-start(f32[6,2,1024]{2,0,1:T(8,128)} %copy.752), channel_id=1, source_target_pairs={{48,0},{49,1},{50,2},{51,3},{52,4},{53,5},{54,6},{55,7},{56,8},{57... | collective-permute-start | bytes 147464 | tf_op jit(solution)/shard_map/ppermute | solution.py:22
  434.6 32.6 %collective-permute-start.21 = (f32[6,2,1024]{2,0,1:T(8,128)}, f32[6,2,1024]{2,0,1:T(8,128)}, u32[]{:S(2)}, u32[]{:S(2)}) collective-permute-start(f32[6,2,1024]{2,0,1:T(8,128)} %copy.754), channel_id=1, source_target_pairs={{64,0},{128,64},{192,128},{0,192},{65,1},{129,65},{193,129},{1,193... | collective-permute-start | bytes 147464 | tf_op jit(solution)/shard_map/ppermute | solution.py:22
  451.6 17.8 %collective-permute-start.22 = (f32[6,2,1024]{2,0,1:T(8,128)}, f32[6,2,1024]{2,0,1:T(8,128)}, u32[]{:S(2)}, u32[]{:S(2)}) collective-permute-start(f32[6,2,1024]{2,0,1:T(8,128)} %copy.756), channel_id=1, source_target_pairs={{192,0},{0,64},{64,128},{128,192},{193,1},{1,65},{65,129},{129,193... | collective-permute-start | bytes 147464 | tf_op jit(solution)/shard_map/ppermute | solution.py:22
  458.1 28.8 %collective-permute-start.63 = (f32[2,1024]{1,0:T(2,128)S(1)}, f32[2,1024]{1,0:T(2,128)S(1)}, u32[]{:S(2)}, u32[]{:S(2)}) collective-permute-start(f32[2,1024]{1,0:T(2,128)S(1)} %reshape_squeeze.162), channel_id=1, source_target_pairs={{64,0},{128,64},{192,128},{0,192},{65,1},{129,65},{193,129},{1,193... | collective-permute-start | bytes 24584 | tf_op jit(solution)/shard_map/ppermute | solution.py:22
  472.5 15.9 %collective-permute-start.61 = (f32[2,1024]{1,0:T(2,128)S(1)}, f32[2,1024]{1,0:T(2,128)S(1)}, u32[]{:S(2)}, u32[]{:S(2)}) collective-permute-start(f32[2,1024]{1,0:T(2,128)S(1)} %reshape_squeeze.160), channel_id=1, source_target_pairs={{16,0},{17,1},{18,2},{19,3},{20,4},{21,5},{22,6},{23,7},{24,8},{25... | collective-permute-start | bytes 24584 | tf_op jit(solution)/shard_map/ppermute | solution.py:22
  473.8 18.8 %collective-permute-start.62 = (f32[2,1024]{1,0:T(2,128)}, f32[2,1024]{1,0:T(2,128)S(1)}, u32[]{:S(2)}, u32[]{:S(2)}) collective-permute-start(f32[2,1024]{1,0:T(2,128)} %reshape_squeeze.161), channel_id=1, source_target_pairs={{48,0},{49,1},{50,2},{51,3},{52,4},{53,5},{54,6},{55,7},{56,8},{57... | collective-permute-start | bytes 24584 | tf_op jit(solution)/shard_map/ppermute | solution.py:22
  514.5 16.9 %collective-permute-start.69 = (f32[2,1024]{1,0:T(2,128)S(1)}, f32[2,1024]{1,0:T(2,128)S(1)}, u32[]{:S(2)}, u32[]{:S(2)}) collective-permute-start(f32[2,1024]{1,0:T(2,128)S(1)} %reshape_squeeze.166), channel_id=1, source_target_pairs={{64,0},{128,64},{192,128},{0,192},{65,1},{129,65},{193,129},{1,193... | collective-permute-start | bytes 24584 | tf_op jit(solution)/shard_map/ppermute | solution.py:22
  518.9 18.2 %collective-permute-start.68 = (f32[2,1024]{1,0:T(2,128)}, f32[2,1024]{1,0:T(2,128)S(1)}, u32[]{:S(2)}, u32[]{:S(2)}) collective-permute-start(f32[2,1024]{1,0:T(2,128)} %reshape_squeeze.165), channel_id=1, source_target_pairs={{48,0},{49,1},{50,2},{51,3},{52,4},{53,5},{54,6},{55,7},{56,8},{57... | collective-permute-start | bytes 24584 | tf_op jit(solution)/shard_map/ppermute | solution.py:22
  556.4 20.9 %collective-permute-start.71 = (f32[2,1024]{1,0:T(2,128)S(1)}, f32[2,1024]{1,0:T(2,128)S(1)}, u32[]{:S(2)}, u32[]{:S(2)}) collective-permute-start(f32[2,1024]{1,0:T(2,128)S(1)} %get-tuple-element.842), channel_id=1, source_target_pairs={{1,0},{2,1},{3,2},{4,3},{5,4},{6,5},{7,6},{8,7},{9,8},{10,9},{11,1... | collective-permute-start | bytes 24584 | tf_op jit(solution)/shard_map/ppermute | solution.py:22
  682.4 18.3 %collective-permute-start.2 = (f32[6,32,1024]{2,1,0:T(8,128)S(1)}, f32[6,32,1024]{2,1,0:T(8,128)}, u32[]{:S(2)}, u32[]{:S(2)}) collective-permute-start(f32[6,32,1024]{2,1,0:T(8,128)S(1)} %get-tuple-element.313), channel_id=1, source_target_pairs={{0,64},{1,65},{2,66},{3,67},{4,68},{5,69},{6,70},{7,71},{8,72},{9,... | collective-permute-start | bytes 2359304 | tf_op jit(solution)/shard_map/cond/branch_1_fun/ppermute | solution.py:28
  (110 other events, 3235.1 us)
where the time goes:
time: 732 us; the launch traced here: 722 us
  local copies, waits for them, and re-layouts  353 us (48%)
  other arithmetic  123 us (17%)
  starting transfers between devices  92.2 us (13%)
  blocking collectives  78.6 us (11%)
  waiting for transfers between devices  64.8 us (9%)
  between operations  9.13 us (1%)
    ppermute x66, starting transfers between devices, passed_along(): return lax.ppermute(block, axis, route)  88.5 us
    pmax x1, blocking collectives, local(): used = lax.pmax(flags, ('group', 'dev'))  78.6 us
    gather x66, local copies, waits for them, and re-layouts, collect_halos(): jnp.take(payload, chosen, axis=-2)  53.6 us
    div x16, other arithmetic, relax(): return total / (6.0 + screening)  52.1 us
    ppermute x66, waiting for transfers between devices, passed_along(): return lax.ppermute(block, axis, route)  47.6 us
    dynamic_update_slice x6, other arithmetic, local_update(): lax.map(ion_update, (species, stacked_halos, half_charge, diffusivity, si...  29.4 us
    dynamic_slice x18, local copies, waits for them, and re-layouts, local_update(): lax.map(ion_update, (species, stacked_halos, half_charge, diffusivity, si...  23 us
    concatenate x20, local copies, waits for them, and re-layouts, beside_values(): jnp.concatenate([field[..., 1:], field[..., :1]], axis=-1)  17.9 us
  transfers between devices with their start and end apart: 70, of which 20 were waited for; matrix products, arithmetic and copies ran while one was open for 43% of the time, Pallas kernels for 0%

commit v1 on v0

v1 whole, which is shorter than its diff:
```python
from functools import partial

import jax
import jax.numpy as jnp
from jax import lax
from jax.experimental import pallas as pl
from jax.experimental.pallas import tpu as pltpu
from jax.sharding import PartitionSpec as P

MESH = pl.DeviceIdType.MESH

SIDE = 32
SWEEPS = 8
ROWS = 512
PAD = 16
N_GROUP = 4
N_DEV = 64

charge_scale = 0.5
screening = 0.5
solubility = 2.0
valences = (2.0, -1.0, 1.0, -1.0, 1.0, 2.0)
reaction_signs = (1.0, 1.0, -1.0, 0.0, 0.0, 0.0)
IONS = len(valences)
FIELDS = IONS + 1
INV = 1.0 / (6.0 + screening)


def iotas():
    row = lax.broadcasted_iota(jnp.int32, (8, 128), 0)
    lane = lax.broadcasted_iota(jnp.int32, (8, 128), 1)
    return row, lane


def lroll(v, shift):
    if isinstance(shift, int):
        shift %= 128
        return v if shift == 0 else pltpu.roll(v, shift, 1)
    return pltpu.roll(v, shift, 1)


def sroll(v, shift):
    shift %= 8
    return v if shift == 0 else pltpu.roll(v, shift, 0)


def flipped(group, dev, bit):
    q = group * N_DEV + dev
    mask = 2**bit
    other = q + (1 - 2 * ((q // mask) % 2)) * mask
    return {"group": other // N_DEV, "dev": other % N_DEV}


def plane_rows(x):
    return pl.multiple_of(x * 16, 16)


def pack_start():
    zero = jnp.zeros((8, 128), jnp.float32)
    return (zero,) * 8


def pack_planes(acc, xi, planes, row, lane):
    acc = list(acc)
    for j in range(2):
        low = high = None
        for i in range(4):
            a, b = planes[4 * j + i]
            first, last = sroll(a, 2 * i), sroll(b, 2 * i - 6)
            low = first if low is None else jnp.where(row // 2 == i, first, low)
            high = last if high is None else jnp.where(row // 2 == i, last, high)
        here = lane // 32 == xi
        acc[j] = jnp.where(here, lroll(low, 32 * xi), acc[j])
        acc[2 + j] = jnp.where(here, lroll(high, (32 * xi + 32) % 128), acc[2 + j])
    for i in range(8):
        x = 4 * i + xi
        z0, z1 = lane % 32 == x, lane % 32 == (x + 31) % 32
        for h in range(2):
            turned = lroll(planes[i][h], x)
            acc[4 + h] = jnp.where(z0, turned, acc[4 + h])
            acc[6 + h] = jnp.where(z1, turned, acc[6 + h])
    return tuple(acc)


def pack_end(acc):
    return acc[:6] + (lroll(acc[6], 97), lroll(acc[7], 97))


def around(a, b, x, i, turned, above, below, row, lane):
    north, south = turned
    ra, rb = lroll(a, 96), lroll(b, 96)
    ua, ub = sroll(ra, 6), sroll(rb, 6)
    edge = sroll(north[i // 4], 6 - 2 * (i % 4))
    na = jnp.where(lane < 96, ra, jnp.where(row < 6, ua, ub))
    nb = jnp.where(lane < 96, rb, jnp.where(row < 6, ub, edge))
    qa, qb = lroll(a, 32), lroll(b, 32)
    da, db = sroll(qa, 2), sroll(qb, 2)
    edge = sroll(south[i // 4], -2 * (i % 4))
    sa = jnp.where(lane >= 32, qa, jnp.where(row >= 2, da, edge))
    sb = jnp.where(lane >= 32, qb, jnp.where(row >= 2, db, da))
    top, bottom = lane % 32 == 31, lane % 32 == 0
    up = [jnp.where(top, lroll(above[h], 31 - x), lroll(v, 127)) for h, v in enumerate((a, b))]
    down = [
        jnp.where(bottom, lroll(below[h], (128 - x) % 128), lroll(v, 1)) for h, v in enumerate((a, b))
    ]
    return (na, sa, up[0], down[0]), (nb, sb, up[1], down[1])


def turn_faces(faces, xi):
    north = [lroll(v, (96 + 128 - 32 * xi) % 128) for v in faces[0]]
    south = [lroll(v, (128 - 32 * xi) % 128) for v in faces[1]]
    return north, south


def step_kernel(
    potential,
    pore,
    openness,
    species,
    neighbours,
    diffusivity,
    rate_const,
    opened,
    partner,
    give_slot,
    updated,
    outgoing,
    choice,
    phi,
    conc,
    near,
    dens,
    pore_in,
    open_in,
    packed,
    arrived,
    packed_all,
    arrived_all,
    flag,
    flag_in,
    load_sems,
    send_sems,
    recv_sems,
    send_all_sems,
    recv_all_sems,
    flag_send,
    flag_recv,
):
    row, lane = iotas()
    even = row % 2 == 0
    group, dev = lax.axis_index("group"), lax.axis_index("dev")
    loads = [
        pltpu.make_async_copy(potential, phi.at[0, pl.ds(PAD, ROWS)], load_sems.at[0]),
        pltpu.make_async_copy(pore, pore_in, load_sems.at[1]),
        pltpu.make_async_copy(openness, open_in, load_sems.at[2]),
    ] + [
        pltpu.make_async_copy(species.at[i], conc.at[i, pl.ds(PAD, ROWS)], load_sems.at[3 + i])
        for i in range(IONS)
    ]
    for load in loads:
        load.start()

    targets = [
        {"dev": (dev + N_DEV - 1) % N_DEV},
        {"dev": (dev + 1) % N_DEV},
        {"dev": (dev + N_DEV - 16) % N_DEV},
        {"dev": (dev + 16) % N_DEV},
        {"group": (group + N_GROUP - 1) % N_GROUP},
        {"group": (group + 1) % N_GROUP},
    ]
    flips = [flipped(group, dev, bit) for bit in range(8)]
    barrier = pltpu.get_barrier_semaphore()
    for target in targets + flips:
        pl.semaphore_signal(barrier, inc=1, device_id=target, device_id_type=MESH)

    keep = []
    for k in range(6):
        slots = jnp.where(even, neighbours[0, k], neighbours[1, k])
        keep.append(slots == row % 2)

    def chosen(k, v):
        return jnp.where(keep[k], v, jnp.where(even, sroll(v, 7), sroll(v, 1)))

    def chosen_face(ref, k):
        return [chosen(k, ref[0:8, :]), chosen(k, ref[8:16, :])]

    zeros = jnp.zeros((PAD, 128), jnp.float32)
    for s in range(2):
        phi[s, 0:PAD, :] = zeros
        phi[s, PAD + ROWS : PAD + ROWS + PAD, :] = zeros

    def sends(state):
        slot = state % 2
        sources = [phi.at[slot, pl.ds(PAD, 16)], phi.at[slot, pl.ds(ROWS, 16)]] + [
            packed.at[state, k - 2] for k in range(2, 6)
        ]
        return [
            pltpu.make_async_remote_copy(
                src_ref=sources[k],
                dst_ref=arrived.at[state, k],
                send_sem=send_sems.at[state, k],
                recv_sem=recv_sems.at[state, k],
                device_id=targets[k],
                device_id_type=MESH,
            )
            for k in range(6)
        ]

    def put_faces(ref_of, acc):
        for k in range(4):
            ref = ref_of(k)
            ref[0:8, :] = acc[2 * k]
            ref[8:16, :] = acc[2 * k + 1]

    def pack_field(read):
        def step(xi, acc):
            planes = []
            for i in range(8):
                r = plane_rows(4 * i + xi) + PAD
                planes.append((read(r), read(r + 8)))
            return pack_planes(acc, xi, planes, row, lane)

        return pack_end(lax.fori_loop(0, 4, step, pack_start()))

    loads[0].wait()
    acc = pack_field(lambda r: phi[0, pl.ds(pl.multiple_of(r, 8), 8), :])
    put_faces(lambda k: packed.at[0, k], acc)
    me = group * N_DEV + dev
    flag[0] = jnp.where(
        lane < 8,
        jnp.where(
            jnp.bitwise_xor(partner[0], me) == lax.shift_left(jnp.ones_like(lane), lane % 8), 1.0, 0.0
        ),
        0.0,
    )
    pl.semaphore_wait(barrier, len(targets) + len(flips))
    for copy in sends(0):
        copy.start()

    for load in loads[1:]:
        load.wait()

    def prepare(x, carry):
        for h in range(2):
            r = pl.multiple_of(x * 16 + 8 * h, 8)
            rows, inner = pl.ds(r, 8), pl.ds(pl.multiple_of(r + PAD, 8), 8)
            wet = pore_in[rows, :].astype(jnp.float32) * open_in[rows, :]
            conc[IONS, inner, :] = wet
            total = valences[0] * conc[0, inner, :]
            for i in range(1, IONS):
                total = total + valences[i] * conc[i, inner, :]
            dens[rows, :] = (charge_scale * INV) * wet * total
        return carry

    lax.fori_loop(0, SIDE, prepare, 0)

    def pack_one(f, carry):
        acc = pack_field(lambda r: conc[f, pl.ds(pl.multiple_of(r, 8), 8), :])
        put_faces(lambda k: packed_all.at[k, f], acc)
        return carry

    lax.fori_loop(0, FIELDS, pack_one, 0)
    sources = [conc.at[:, pl.ds(PAD, 16)], conc.at[:, pl.ds(ROWS, 16)]] + [
        packed_all.at[k] for k in range(4)
    ]
    all_sends = [
        pltpu.make_async_remote_copy(
            src_ref=sources[k],
            dst_ref=arrived_all.at[k],
            send_sem=send_all_sems.at[k],
            recv_sem=recv_all_sems.at[k],
            device_id=targets[k],
            device_id_type=MESH,
        )
        for k in range(6)
    ]
    for copy in all_sends:
        copy.start()

    def flag_copy(bit):
        return pltpu.make_async_remote_copy(
            src_ref=flag.at[bit],
            dst_ref=flag_in.at[bit],
            send_sem=flag_send.at[bit],
            recv_sem=flag_recv.at[bit],
            device_id=flips[bit],
            device_id_type=MESH,
        )

    def near_field(f, read, halo):
        faces = [chosen_face(halo(k), k) for k in range(2, 6)]

        def step(xi, carry):
            turned = turn_faces(faces[:2], xi)
            for i in range(8):
                x = 4 * i + xi
                r = plane_rows(x)
                a, b = read(r + PAD), read(r + PAD + 8)
                both = around(a, b, x, i, turned, faces[2], faces[3], row, lane)
                for h in range(2):
                    rows = pl.ds(pl.multiple_of(r + 8 * h, 8), 8)
                    for n in range(4):
                        near[f, n, rows, :] = both[h][n]
            return carry

        lax.fori_loop(0, 4, step, 0)

    def sweep(t, carry):
        old, new = t % 2, (t + 1) % 2
        for bit in range(8):

            @pl.when(t == bit)
            def _(bit=bit):
                flag_copy(bit).start()

        copies = sends(t)
        for k in range(2, 6):
            copies[k].wait_recv()
        faces = [chosen_face(arrived.at[t, k], k) for k in range(2, 6)]

        def read(r):
            return phi[old, pl.ds(pl.multiple_of(r, 8), 8), :]

        def step(xi, acc):
            turned = turn_faces(faces[:2], xi)
            planes = []
            for i in range(8):
                x = 4 * i + xi
                r = plane_rows(x)
                a, b = read(r + PAD), read(r + PAD + 8)
                both = around(a, b, x, i, turned, faces[2], faces[3], row, lane)
                out = []
                for h in range(2):
                    rows = pl.ds(pl.multiple_of(r + 8 * h, 8), 8)
                    total = read(r + 8 * h) + read(r + 8 * h + 2 * PAD)
                    for value in both[h]:
                        total = total + value
                    value = total * INV + dens[rows, :]
                    phi[new, pl.ds(pl.multiple_of(r + 8 * h + PAD, 8), 8), :] = value
                    out.append(value)
                planes.append(tuple(out))
            return pack_planes(acc, xi, planes, row, lane)

        acc = list(pack_end(lax.fori_loop(0, 4, step, pack_start())))
        for k in range(2):
            copies[k].wait_recv()
        for copy in copies:
            copy.wait_send()
        ends = []
        for k, base in ((1, PAD), (0, ROWS)):
            halo = chosen_face(arrived.at[t, k], k)
            pair = []
            for h in range(2):
                value = phi[new, base + 8 * h : base + 8 * h + 8, :] + halo[h] * INV
                phi[new, base + 8 * h : base + 8 * h + 8, :] = value
                pair.append(value)
            ends.append(pair)
        (fa, fb), (la, lb) = ends
        first = (row < 2) & (lane < 32)
        last = (row >= 6) & (lane >= 96)
        acc[0] = jnp.where(first, fa, acc[0])
        acc[2] = jnp.where(first, lroll(sroll(fb, 2), 32), acc[2])
        acc[1] = jnp.where(last, lroll(sroll(la, 6), 96), acc[1])
        acc[3] = jnp.where(last, lb, acc[3])
        for h in range(2):
            acc[4 + h] = jnp.where(lane % 32 == 0, (fa, fb)[h], acc[4 + h])
            acc[4 + h] = jnp.where(lane % 32 == 31, lroll((la, lb)[h], 31), acc[4 + h])
            acc[6 + h] = jnp.where(lane % 32 == 0, lroll((fa, fb)[h], 97), acc[6 + h])
            acc[6 + h] = jnp.where(lane % 32 == 31, (la, lb)[h], acc[6 + h])
        put_faces(lambda k: packed.at[t + 1, k], acc)
        for copy in sends(t + 1):
            copy.start()

        @pl.when(t == 0)
        def _():
            for copy in all_sends:
                copy.wait()

        @pl.when(t > 0)
        def _():
            f = t - 1
            near_field(
                f,
                lambda r: conc[f, pl.ds(pl.multiple_of(r, 8), 8), :],
                lambda k: arrived_all.at[k, f],
            )
            conc[f, 0:PAD, :] = jnp.concatenate(chosen_face(arrived_all.at[1, f], 1), axis=0)
            conc[f, PAD + ROWS : PAD + ROWS + PAD, :] = jnp.concatenate(
                chosen_face(arrived_all.at[0, f], 0), axis=0
            )

        for bit in range(8):

            @pl.when(t == bit)
            def _(bit=bit):
                flag_copy(bit).wait()

        flag[t + 1] = jnp.maximum(flag[t], flag_in[t])
        return carry

    lax.fori_loop(0, SWEEPS, sweep, 0)

    used = flag[SWEEPS]

    def bit_used(bit):
        return jnp.max(jnp.where(lane == bit, used, 0.0))

    inner = 0.0
    inner_any = 0.0
    for bit in range(6):
        on = bit_used(bit)
        inner = inner + on * bit
        inner_any = inner_any + on
    pick = jnp.where(inner_any > 0.0, 2.0 * inner + bit_used(7), 12.0)
    choice[0] = pick.astype(jnp.int32)

    copies = sends(SWEEPS)
    for k in range(2, 6):
        copies[k].wait_recv()
    near_field(
        FIELDS,
        lambda r: phi[0, pl.ds(pl.multiple_of(r, 8), 8), :],
        lambda k: arrived.at[SWEEPS, k],
    )
    activity = jnp.where(
        even,
        rate_const[0] * opened[0].astype(jnp.float32),
        rate_const[1] * opened[1].astype(jnp.float32),
    )
    give_first = jnp.full((8, 128), give_slot[0], jnp.int32) == 0
    rates = [diffusivity[i] for i in range(IONS)]

    def finish(x, carry):
        halves = []
        for h in range(2):
            r = pl.multiple_of(x * 16 + 8 * h, 8)
            rows = pl.ds(r, 8)
            inner_rows = pl.ds(pl.multiple_of(r + PAD, 8), 8)
            after = pl.ds(pl.multiple_of(r + 2 * PAD, 8), 8)

            def six(f, ref):
                return [ref(after), ref(rows)] + [near[f, n, rows, :] for n in range(4)]

            wet = conc[IONS, inner_rows, :]
            swept = phi[0, inner_rows, :]
            near_wet = six(IONS, lambda s: conc[IONS, s, :])
            near_swept = six(FIELDS, lambda s: phi[0, s, :])
            flow = drift = None
            weights = {1.0: [], 0.5: [], -0.5: []}
            for n in range(6):
                g = wet * near_wet[n]
                d = g * (swept - near_swept[n])
                half = 0.5 * d
                flow = g if flow is None else flow + g
                drift = d if drift is None else drift + d
                weights[1.0].append(g - d)
                weights[0.5].append(g - half)
                weights[-0.5].append(g + half)
            totals = {half: flow + half * drift for half in weights}
            ions = [conc[i, inner_rows, :] for i in range(IONS)]
            reaction = (
                activity
                * pore_in[rows, :].astype(jnp.float32)
                * (ions[2] - ions[0] * ions[1] * (1.0 / solubility))
            )
            out = []
            for i in range(IONS):
                half = 0.5 * valences[i]
                neighbours_of = six(i, lambda s, i=i: conc[i, s, :])
                outflow = ions[i] * totals[half]
                for n in range(6):
                    outflow = outflow - weights[half][n] * neighbours_of[n]
                value = ions[i] - rates[i] * outflow
                if reaction_signs[i] > 0:
                    value = value + reaction
                elif reaction_signs[i] < 0:
                    value = value - reaction
                updated[i, rows, :] = value
                out.append(value)
            updated[IONS, rows, :] = swept
            out.append(swept)
            halves.append(out)
        for i in range(FIELDS):
            a, b = halves[0][i], halves[1][i]
            outgoing[i, pl.ds(pl.multiple_of(x * 8, 8), 8), :] = jnp.where(
                even,
                jnp.where(give_first, a, sroll(a, 7)),
                jnp.where(give_first, sroll(b, 1), b),
            )
        return carry

    lax.fori_loop(1, SIDE - 1, finish, 0)
    for k in range(2):
        copies[k].wait_recv()
    for copy in copies:
        copy.wait_send()
    phi[0, 0:PAD, :] = jnp.concatenate(chosen_face(arrived.at[SWEEPS, 1], 1), axis=0)
    phi[0, PAD + ROWS : PAD + ROWS + PAD, :] = jnp.concatenate(
        chosen_face(arrived.at[SWEEPS, 0], 0), axis=0
    )
    lax.fori_loop(0, 2, lambda s, carry: finish(s * (SIDE - 1), carry), 0)


PAIRS = tuple((inner, outer) for inner in range(6) for outer in (6, 7)) + ((6, 7),)


def exchange_kernel(bits, outgoing, received, send_sems, recv_sems):
    group, dev = lax.axis_index("group"), lax.axis_index("dev")
    targets = [flipped(group, dev, bit) for bit in bits]
    barrier = pltpu.get_barrier_semaphore()
    for target in targets:
        pl.semaphore_signal(barrier, inc=1, device_id=target, device_id_type=MESH)
    pl.semaphore_wait(barrier, 2)
    copies = [
        pltpu.make_async_remote_copy(
            src_ref=outgoing.at[i],
            dst_ref=received.at[j, i],
            send_sem=send_sems.at[j, i],
            recv_sem=recv_sems.at[j, i],
            device_id=targets[j],
            device_id_type=MESH,
        )
        for i in range(FIELDS)
        for j in range(2)
    ]
    for copy in copies:
        copy.start()
    for copy in copies:
        copy.wait()


def exchange(outgoing, number):
    return pl.pallas_call(
        partial(exchange_kernel, PAIRS[number]),
        out_shape=jax.ShapeDtypeStruct((2, FIELDS, ROWS // 2, 128), jnp.float32),
        in_specs=[pl.BlockSpec(memory_space=pl.ANY)],
        out_specs=pl.BlockSpec(memory_space=pl.ANY),
        scratch_shapes=[pltpu.SemaphoreType.DMA((2, FIELDS))] * 2,
        compiler_params=pltpu.CompilerParams(collective_id=1 + number, has_side_effects=True),
        name=f"exchange_{number}",
    )(outgoing)


def merge_kernel(updated, received, control, new_species, new_potential):
    row, _ = iotas()
    even = row % 2 == 0
    first = control[0]
    give = control[1]
    swapped = control[2]
    give_first = jnp.full((8, 128), give, jnp.int32) == 0
    mine = (jnp.full((8, 128), swapped, jnp.int32) > 0) & (row % 2 == jnp.full((8, 128), give, jnp.int32))
    take_first = jnp.full((8, 128), first, jnp.int32) > 0

    def step(x, carry):
        for i in range(FIELDS):
            rows = pl.ds(pl.multiple_of(x * 8, 8), 8)
            got = jnp.where(take_first, received[0, i, rows, :], received[1, i, rows, :])
            halves = (
                jnp.where(give_first, got, sroll(got, 1)),
                jnp.where(give_first, sroll(got, 7), got),
            )
            for h in range(2):
                r = pl.ds(pl.multiple_of(x * 16 + 8 * h, 8), 8)
                value = jnp.where(mine, halves[h], updated[i, r, :])
                if i < IONS:
                    new_species[i, r, :] = value
                else:
                    new_potential[r, :] = value
        return carry

    lax.fori_loop(0, SIDE, step, 0)


def as_rows(field):
    lead = field.shape[:-2]
    split = field.reshape(lead + (2, ROWS // 2, 128))
    return jnp.swapaxes(split, -3, -2).reshape(lead + (ROWS, 128))


def as_bricks(rows):
    lead = rows.shape[:-2]
    split = rows.reshape(lead + (ROWS // 2, 2, 128))
    return jnp.swapaxes(split, -3, -2).reshape(lead + (2, ROWS // 2 * 128))


def local(
    species, potential, pore, openness, neighbours, diffusivity, rate_const, opened, partner, give_slot
):
    any_space = pl.BlockSpec(memory_space=pl.ANY)
    vmem = pl.BlockSpec(memory_space=pltpu.VMEM)
    smem = pl.BlockSpec(memory_space=pltpu.SMEM)
    f32 = jnp.float32
    padded = ROWS + 2 * PAD
    updated, outgoing, choice = pl.pallas_call(
        step_kernel,
        out_shape=(
            jax.ShapeDtypeStruct((FIELDS, ROWS, 128), f32),
            jax.ShapeDtypeStruct((FIELDS, ROWS // 2, 128), f32),
            jax.ShapeDtypeStruct((1,), jnp.int32),
        ),
        in_specs=[any_space] * 4 + [smem] * 6,
        out_specs=(vmem, vmem, smem),
        scratch_shapes=[
            pltpu.VMEM((2, padded, 128), f32),
            pltpu.VMEM((FIELDS, padded, 128), f32),
            pltpu.VMEM((FIELDS + 1, 4, ROWS, 128), f32),
            pltpu.VMEM((ROWS, 128), f32),
            pltpu.VMEM((ROWS, 128), jnp.int32),
            pltpu.VMEM((ROWS, 128), f32),
            pltpu.VMEM((SWEEPS + 1, 4, 16, 128), f32),
            pltpu.VMEM((SWEEPS + 1, 6, 16, 128), f32),
            pltpu.VMEM((4, FIELDS, 16, 128), f32),
            pltpu.VMEM((6, FIELDS, 16, 128), f32),
            pltpu.VMEM((SWEEPS + 1, 8, 128), f32),
            pltpu.VMEM((SWEEPS, 8, 128), f32),
            pltpu.SemaphoreType.DMA((3 + IONS,)),
            pltpu.SemaphoreType.DMA((SWEEPS + 1, 6)),
            pltpu.SemaphoreType.DMA((SWEEPS + 1, 6)),
            pltpu.SemaphoreType.DMA((6,)),
            pltpu.SemaphoreType.DMA((6,)),
            pltpu.SemaphoreType.DMA((SWEEPS,)),
            pltpu.SemaphoreType.DMA((SWEEPS,)),
        ],
        compiler_params=pltpu.CompilerParams(collective_id=0, has_side_effects=True),
        name="step",
    )(
        as_rows(potential),
        as_rows(pore),
        as_rows(openness),
        as_rows(species),
        neighbours,
        diffusivity,
        rate_const,
        opened,
        partner,
        give_slot,
    )
    received = lax.switch(
        choice[0], [partial(exchange, number=number) for number in range(len(PAIRS))], outgoing
    )
    me = lax.axis_index("group") * N_DEV + lax.axis_index("dev")
    apart = jnp.bitwise_xor(partner[0], me)
    first = (apart < 64) | ((apart == 64) & (choice[0] == len(PAIRS) - 1))
    control = jnp.stack([first.astype(jnp.int32), give_slot[0], (apart != 0).astype(jnp.int32)])
    new_species, new_potential = pl.pallas_call(
        merge_kernel,
        out_shape=(
            jax.ShapeDtypeStruct((IONS, ROWS, 128), f32),
            jax.ShapeDtypeStruct((ROWS, 128), f32),
        ),
        in_specs=[vmem, vmem, smem],
        out_specs=(vmem, vmem),
        name="merge",
    )(updated, received, control)
    return as_bricks(new_species), as_bricks(new_potential)


def solution(mesh):
    in_specs = (
        P(None, ("group", "dev"), None),
        P(("group", "dev"), None),
        P(("group", "dev"), None),
        P(("group", "dev"), None),
        P(("group", "dev"), None),
        P(),
        P(("group", "dev")),
        P(("group", "dev")),
        P(("group", "dev")),
        P(("group", "dev")),
    )
    out_specs = (P(None, ("group", "dev"), None), P(("group", "dev"), None))
    return jax.shard_map(local, mesh=mesh, in_specs=in_specs, out_specs=out_specs, check_vma=False)
```

time: 732 us -> 99.9 us (0.14); the launches traced: 722 us -> 101 us
  local copies, waits for them, and re-layouts: 353 us -> 0 us
  other arithmetic: 123 us -> 0.65 us
  Pallas kernels: 0 us -> 96.8 us
  starting transfers between devices: 92.2 us -> 0 us
  blocking collectives: 78.6 us -> 0 us
  waiting for transfers between devices: 64.8 us -> 0 us
    concatenate x118 -> x0, local copies, waits for them, and re-layouts: 100 us -> none  [the longest x20 17.9 us: beside_values(): jnp.concatenate([field[..., 1:], field[..., :1]], axis=-1)]
    pallas_call x0 -> x3, Pallas kernels: none -> 96.8 us  [the longest x1 70.5 us: local(): pl.pallas_call(step_kernel, out_shape=(jax.ShapeDtypeStruct((FIELDS, ROWS...]
    ppermute x70 -> x0, starting transfers between devices: 92.2 us -> none  [the longest x66 88.5 us: passed_along(): return lax.ppermute(block, axis, route)]
    pmax x1 -> x0, blocking collectives: 78.6 us -> none  [local(): used = lax.pmax(flags, ('group', 'dev'))]
    slice x71 -> x0, local copies, waits for them, and re-layouts: 66.1 us -> none  [the longest x3 12.1 us: face_list(): cube_view[..., brick_side - 1].reshape(flat_shape)]
    ppermute x70 -> x0, waiting for transfers between devices: 64.8 us -> none  [the longest x66 47.6 us: passed_along(): return lax.ppermute(block, axis, route)]
    gather x66 -> x0, local copies, waits for them, and re-layouts: 53.6 us -> none  [collect_halos(): jnp.take(payload, chosen, axis=-2)]
    div x16 -> x0, other arithmetic: 52.1 us -> none  [relax(): return total / (6.0 + screening)]
  transfers between devices with their start and end apart: 70 -> 0, of which waited for: 20 -> 0; matrix products, arithmetic and copies ran while one was open for 43% -> 0% of each run, Pallas kernels for 0% -> 0%
where the time goes in v1:
time: 99.9 us; the launch traced here: 101 us
  Pallas kernels  96.8 us (97%)
  between operations  3.2 us (3%)
    pallas_call x1, Pallas kernels, local(): pl.pallas_call(step_kernel, out_shape=(jax.ShapeDtypeStruct((FIELDS, ROWS...  70.5 us
    pallas_call x1, Pallas kernels, exchange(): pl.pallas_call(partial(exchange_kernel, PAIRS[number]), out_shape=jax.Sha...  23.1 us
    pallas_call x1, Pallas kernels, local(): pl.pallas_call(merge_kernel, out_shape=(jax.ShapeDtypeStruct((IONS, ROWS,...  3.19 us

profile of v1, /device:TPU:2, one launch (start us, length us, event | category | flops | bytes accessed | tf_op | source)
XLA Modules:
  0.0 100.7 jit_solution(11426318941653442619)
XLA Ops:
  1.9 70.5 %step.1 = (f32[7,512,128]{2,1,0:T(8,128)}, f32[7,256,128]{2,1,0:T(8,128)S(1)}, s32[1]{0:T(128)}) custom-call(f32[512,128]{1,0:T(8,128)} %bitcast.37, s32[512,128]{1,0:T(8,128)} %bitcast.38, f32[512,128]{1,0:T(8,128)} %bitcast.39, f32[6,512,128]{2,1,0:T(8,128)} %bitcast.36, s32[2,6]{1,0:T(2,128)} %neighbours.1, f32[6]{0:T(128)} %diffusivity.1, f32[2]{0:T(128)} %rate_const.1, ...), custom_call_target="tpu_custom_call" | custom-call | tf_op jit(solution)/shard_map/step/pallas_call | solution.py:594
  73.7 0.6 pad_add_fusion.control
  74.4 23.1 %conditional.1 = (f32[2,7,256,128]{3,2,1,0:T(8,128)S(1)}) conditional(s32[]{:T(128)} %bitcast.12, f32[7,256,128]{2,1,0:T(8,128)S(1)} %get-tuple-element.36, f32[7,256,128]{2,1,0:T(8,128)S(1)} %get-tuple-element.36, f32[7,256,128]{2,1,0:T(8,128)S(1)} %get-tuple-element.36, ...), branch_computations={%region_0.0_spmd, %region_1.0_spmd, %region_2.0_spmd, %region_3.0_... | conditional | bytes 8 | solution.py:638
  74.4 23.1 %exchange_0.1 = f32[2,7,256,128]{3,2,1,0:T(8,128)S(1)} custom-call(f32[7,256,128]{2,1,0:T(8,128)S(1)} %outgoing), custom_call_target="tpu_custom_call" | custom-call | tf_op jit(solution)/shard_map/cond/branch_0_fun/exchange_0/pallas_call | solution.py:533
  97.5 3.2 %merge.1 = (f32[6,512,128]{2,1,0:T(8,128)}, f32[512,128]{1,0:T(8,128)}) custom-call(f32[7,512,128]{2,1,0:T(8,128)} %get-tuple-element.34.updated, f32[2,7,256,128]{3,2,1,0:T(8,128)S(1)} %get-tuple-element.39.received, s32[3]{0:T(128)} %pad_add_fusion.control), custom_call_target="tpu_custom_call" | custom-call | tf_op jit(solution)/shard_map/merge/pallas_call | solution.py:645
